TPU v7x, 32 devices: a whole 2x2x4 slice. The times are simulated.
32 devices in a mesh: dp: 4 (over y, core), ep: 8 (over z, x).
Axes of the slice: x: 2, y: 2, z: 4, core: 2. Of those that a mesh axis runs over, the one named last changes fastest.
Arguments:
- tokens: bfloat16 [32, 256, 2048], P(('dp', 'ep')), may hold values from -6 to 6
- lengths: int32 [32], P(('dp', 'ep')), may hold values from 64 to 256, as said below
- routes: int32 [32, 256, 8], P(('dp', 'ep')), may hold values from 0 to 15, all different within a row
- pair_order: int32 [32, 2048], P(('dp', 'ep')), may hold values from 0 to 2047, each once within a row
- gate_weights: float32 [32, 256, 8], P(('dp', 'ep')), may hold values from 0.05 to 0.5
- attn_weight: bfloat16 [2048, 8192], P(('dp', 'ep')), may hold values from -0.375 to 0.375
- gains: float32 [4352], replicated, may hold values from 0.5 to 1.5
- expert_gate_up: bfloat16 [16, 2048, 2048], P('ep'), may hold values from -0.125 to 0.125
- expert_down: bfloat16 [16, 1024, 2048], P('ep'), may hold values from -0.375 to 0.375
- cotangent: bfloat16 [32, 256, 2048], P(('dp', 'ep')), may hold values from -6 to 6
Outputs:
- output: bfloat16 [32, 256, 2048], P(('dp', 'ep'))
- input_grad: float32 [32, 256, 2048], P(('dp', 'ep'))
- attn_weight_grad: float32 [2048, 8192], P(('dp', 'ep'))
- gains_grad: float32 [4352], P(('dp', 'ep'))
- gate_up_grad: float32 [16, 2048, 2048], P('ep', 'dp')
- down_grad: float32 [16, 1024, 2048], P('ep', 'dp')
Inputs may be any that keep to these rules, and one draw needn't show every extreme that they name: `lengths`: slots at or beyond a sequence's length are padding; in every draw some sequence fills all 256 slots. `routes`: the 8 experts of a slot are distinct. `pair_order`: within each sequence every value appears once.
All inputs are finite; a program needn't handle non-finite values.
Results may differ from a plain program's by a relative error of at most 0.014.
Values may be sent and summed in bfloat16 or wider, within the bound.
No kernel may reach another device: no remote copies, remote signals or barrier semaphores. Data moves between devices by JAX's collectives and lax.ppermute only.
A program may use at most 448 MiB of HBM per device.

v0:
```python
import math
import jax
import jax.numpy as jnp
from jax import lax
from jax.sharding import PartitionSpec as P

HEAD = 128
EPS = 1e-06
THETA = 10000.0
NEG = -1e30


def inv_rms(values):
    return lax.rsqrt(jnp.mean(values * values, axis=-1, keepdims=True) + EPS)


def norm_back(values, inv_scale, gain_vec, grad_in):
    scaled = grad_in * gain_vec
    mean_term = jnp.mean(scaled * values, axis=-1, keepdims=True)
    return inv_scale * scaled - values * (inv_scale * inv_scale * inv_scale) * mean_term


def rope_tables(slot_count, head_size):
    half_size = head_size // 2
    frequency = THETA ** (-(jnp.arange(half_size, dtype=jnp.float32) * 2.0) / head_size)
    angles = jnp.arange(slot_count, dtype=jnp.float32)[:, None] * frequency[None, :]
    return (jnp.cos(angles)[:, None, :], jnp.sin(angles)[:, None, :])


def rotary(values, cosine_table, sine_table):
    half_size = values.shape[-1] // 2
    first_half = values[..., :half_size]
    second_half = values[..., half_size:]
    return jnp.concatenate(
        [
            first_half * cosine_table - second_half * sine_table,
            second_half * cosine_table + first_half * sine_table,
        ],
        axis=-1,
    )


def rotary_back(grad_in, cosine_table, sine_table):
    half_size = grad_in.shape[-1] // 2
    first_half = grad_in[..., :half_size]
    second_half = grad_in[..., half_size:]
    return jnp.concatenate(
        [
            first_half * cosine_table + second_half * sine_table,
            second_half * cosine_table - first_half * sine_table,
        ],
        axis=-1,
    )


def on_device(
    tokens,
    lengths,
    routes,
    pair_order,
    gate_weights,
    attn_weight,
    gains,
    expert_gate_up,
    expert_down,
    cotangent,
):
    slot_count = tokens.shape[1]
    model_width = tokens.shape[2]
    head_size = HEAD
    head_count = model_width // head_size
    top_count = routes.shape[2]
    experts_dev = expert_gate_up.shape[0]
    hidden_units = expert_down.shape[1]
    groups = lax.axis_size("ep")
    experts = experts_dev * groups
    capacity = (9 * slot_count * top_count + 8 * experts - 1) // (8 * experts)
    pair_count = slot_count * top_count
    factor = 1.0 / math.sqrt(head_size)
    inputs = tokens[0].astype(jnp.float32)
    length = lengths[0]
    slot_live = jnp.arange(slot_count) < length
    live_rows = slot_live.astype(jnp.float32)[:, None]
    gain_attn = gains[:model_width]
    gain_ffn = gains[model_width : 2 * model_width]
    gain_query = gains[2 * model_width : 2 * model_width + head_size]
    gain_key = gains[2 * model_width + head_size :]
    whole_weight = lax.all_gather(attn_weight, ("dp", "ep"), axis=0, tiled=True)
    weight_qkv = whole_weight[:, : 3 * model_width]
    weight_out = whole_weight[:, 3 * model_width :]
    scale_first = inv_rms(inputs)
    xn_first = (inputs * scale_first * gain_attn).astype(jnp.bfloat16)
    projected = jnp.dot(xn_first, weight_qkv, preferred_element_type=jnp.float32)
    query_raw = projected[:, :model_width].reshape(slot_count, head_count, head_size)
    key_raw = projected[:, model_width : 2 * model_width].reshape(slot_count, head_count, head_size)
    values_low = (
        projected[:, 2 * model_width :]
        .astype(jnp.bfloat16)
        .reshape(slot_count, head_count, head_size)
    )
    cosine_table, sine_table = rope_tables(slot_count, head_size)
    query_scale = inv_rms(query_raw)
    key_scale = inv_rms(key_raw)
    query_rot = rotary(query_raw * query_scale * gain_query, cosine_table, sine_table).astype(
        jnp.bfloat16
    )
    key_rot = rotary(key_raw * key_scale * gain_key, cosine_table, sine_table).astype(jnp.bfloat16)

    def score_table():
        raw_scores = (
            jnp.einsum("qhd,khd->hqk", query_rot, key_rot, preferred_element_type=jnp.float32)
            * factor
        )
        return jnp.where(slot_live[None, None, :], raw_scores, NEG)

    scores = score_table()
    row_max = jnp.max(scores, axis=-1, keepdims=True)
    log_total = row_max + jnp.log(jnp.sum(jnp.exp(scores - row_max), axis=-1, keepdims=True))
    probs_low = jnp.exp(scores - log_total).astype(jnp.bfloat16)
    attended = jnp.einsum("hqk,khd->qhd", probs_low, values_low, preferred_element_type=jnp.float32)
    attended = attended.reshape(slot_count, model_width).astype(jnp.bfloat16)
    resid = inputs + jnp.dot(attended, weight_out, preferred_element_type=jnp.float32)
    scale_second = inv_rms(resid)
    xn_second = (resid * scale_second * gain_ffn).astype(jnp.bfloat16)
    expert_flat = routes[0].reshape(pair_count)
    order_row = pair_order[0]
    pair_index = jnp.arange(pair_count, dtype=jnp.int32)
    pair_live = pair_index // top_count < length
    by_rank = jnp.zeros((pair_count,), jnp.int32).at[order_row].set(pair_index)
    one_hot = (
        (expert_flat[by_rank][:, None] == jnp.arange(experts, dtype=jnp.int32)[None, :])
        & pair_live[by_rank][:, None]
    ).astype(jnp.int32)
    earlier = jnp.cumsum(one_hot, axis=0) - one_hot
    pair_rank = jnp.sum(earlier * one_hot, axis=1)[order_row]
    kept_pair = pair_live & (pair_rank < capacity)
    dest_slot = jnp.where(kept_pair, expert_flat * capacity + pair_rank, experts * capacity)
    source = (
        jnp.full((experts * capacity + 1,), pair_count, jnp.int32).at[dest_slot].set(pair_index)
    )
    source = source[: experts * capacity]
    source_token = source // top_count
    xn_ext = jnp.concatenate([xn_second, jnp.zeros((1, model_width), jnp.bfloat16)], axis=0)
    send_rows = xn_ext[source_token].reshape(groups, experts_dev, capacity, model_width)
    received = lax.all_to_all(send_rows, "ep", split_axis=0, concat_axis=0, tiled=True)
    gate_up = jnp.einsum(
        "sjcd,jdf->sjcf", received, expert_gate_up, preferred_element_type=jnp.float32
    )
    activation = (jax.nn.silu(gate_up[..., :hidden_units]) * gate_up[..., hidden_units:]).astype(
        jnp.bfloat16
    )
    result = jnp.einsum(
        "sjcf,jfd->sjcd", activation, expert_down, preferred_element_type=jnp.float32
    )
    returned = lax.all_to_all(
        result.astype(jnp.bfloat16), "ep", split_axis=0, concat_axis=0, tiled=True
    )
    returned, received, gate_up, activation = (returned, received, gate_up, activation)
    back_ext = jnp.concatenate(
        [
            returned.reshape(experts * capacity, model_width),
            jnp.zeros((1, model_width), jnp.bfloat16),
        ],
        axis=0,
    )
    weight = jnp.where(kept_pair, gate_weights[0].reshape(pair_count), 0.0)
    mixed = jnp.sum(
        (back_ext[dest_slot].astype(jnp.float32) * weight[:, None]).reshape(
            slot_count, top_count, model_width
        ),
        axis=1,
    )
    output = (live_rows * (resid + mixed)).astype(jnp.bfloat16)
    grad_out = cotangent[0].astype(jnp.float32) * live_rows
    grad_ext = jnp.concatenate([grad_out, jnp.zeros((1, model_width), jnp.float32)], axis=0)
    weight_ext = jnp.concatenate([weight, jnp.zeros((1,), jnp.float32)], axis=0)
    slot_grad = (grad_ext[source_token] * weight_ext[source][:, None]).astype(jnp.bfloat16)
    slot_grad = slot_grad.reshape(groups, experts_dev, capacity, model_width)
    grad_recv = lax.all_to_all(slot_grad, "ep", split_axis=0, concat_axis=0, tiled=True)
    grad_act = jnp.einsum(
        "sjcd,jfd->sjcf", grad_recv, expert_down, preferred_element_type=jnp.float32
    )
    grad_down = jnp.einsum(
        "sjcf,sjcd->jfd", activation, grad_recv, preferred_element_type=jnp.float32
    )
    gate_part = gate_up[..., :hidden_units]
    up_part = gate_up[..., hidden_units:]
    sigmoid_gate = jax.nn.sigmoid(gate_part)
    grad_gate = grad_act * up_part * sigmoid_gate * (1.0 + gate_part * (1.0 - sigmoid_gate))
    grad_up = grad_act * gate_part * sigmoid_gate
    grad_gate_up = jnp.concatenate([grad_gate, grad_up], axis=-1).astype(jnp.bfloat16)
    grad_weight_gu = jnp.einsum(
        "sjcd,sjcf->jdf", received, grad_gate_up, preferred_element_type=jnp.float32
    )
    grad_rows = jnp.einsum(
        "sjcf,jdf->sjcd", grad_gate_up, expert_gate_up, preferred_element_type=jnp.float32
    )
    rows_back = lax.all_to_all(
        grad_rows.astype(jnp.bfloat16), "ep", split_axis=0, concat_axis=0, tiled=True
    )
    rows_ext = jnp.concatenate(
        [
            rows_back.reshape(experts * capacity, model_width),
            jnp.zeros((1, model_width), jnp.bfloat16),
        ],
        axis=0,
    )
    grad_xn_second = jnp.sum(
        rows_ext[dest_slot].astype(jnp.float32).reshape(slot_count, top_count, model_width), axis=1
    )
    expert_sums = (
        lax.psum_scatter(grad_weight_gu, "dp", scatter_dimension=1, tiled=True),
        lax.psum_scatter(grad_down, "dp", scatter_dimension=1, tiled=True),
    )
    grad_resid = grad_out + norm_back(resid, scale_second, gain_ffn, grad_xn_second)
    grad_gain_ffn = jnp.sum(grad_xn_second * resid * scale_second, axis=0)
    grad_branch = grad_resid.astype(jnp.bfloat16)
    grad_wout = jnp.einsum("sa,sb->ab", attended, grad_branch, preferred_element_type=jnp.float32)
    grad_att = jnp.einsum("sb,ab->sa", grad_branch, weight_out, preferred_element_type=jnp.float32)
    grad_att = grad_att.astype(jnp.bfloat16).reshape(slot_count, head_count, head_size)
    scores_again = score_table()
    probs_again = jnp.exp(scores_again - log_total)
    grad_probs = jnp.einsum(
        "qhd,khd->hqk", grad_att, values_low, preferred_element_type=jnp.float32
    )
    grad_values = jnp.einsum(
        "hqk,qhd->khd",
        probs_again.astype(jnp.bfloat16),
        grad_att,
        preferred_element_type=jnp.float32,
    )
    grad_values = grad_values.astype(jnp.bfloat16)
    inner_sum = jnp.sum(probs_again * grad_probs, axis=-1, keepdims=True)
    grad_scores = (probs_again * (grad_probs - inner_sum)).astype(jnp.bfloat16)
    grad_qrot = (
        jnp.einsum("hqk,khd->qhd", grad_scores, key_rot, preferred_element_type=jnp.float32)
        * factor
    )
    grad_krot = (
        jnp.einsum("hqk,qhd->khd", grad_scores, query_rot, preferred_element_type=jnp.float32)
        * factor
    )
    grad_qnorm = rotary_back(grad_qrot, cosine_table, sine_table)
    grad_knorm = rotary_back(grad_krot, cosine_table, sine_table)
    grad_query = norm_back(query_raw, query_scale, gain_query, grad_qnorm).astype(jnp.bfloat16)
    grad_key = norm_back(key_raw, key_scale, gain_key, grad_knorm).astype(jnp.bfloat16)
    grad_gain_query = jnp.sum(grad_qnorm * query_raw * query_scale, axis=(0, 1))
    grad_gain_key = jnp.sum(grad_knorm * key_raw * key_scale, axis=(0, 1))
    grad_proj = jnp.concatenate(
        [
            grad_query.reshape(slot_count, model_width),
            grad_key.reshape(slot_count, model_width),
            grad_values.reshape(slot_count, model_width),
        ],
        axis=1,
    )
    grad_wqkv = jnp.einsum("sa,sb->ab", xn_first, grad_proj, preferred_element_type=jnp.float32)
    grad_xn_first = jnp.einsum(
        "sb,ab->sa", grad_proj, weight_qkv, preferred_element_type=jnp.float32
    )
    input_grad = grad_resid + norm_back(inputs, scale_first, gain_attn, grad_xn_first)
    grad_gain_attn = jnp.sum(grad_xn_first * inputs * scale_first, axis=0)
    gain_terms = jnp.concatenate(
        [grad_gain_attn, grad_gain_ffn, grad_gain_query, grad_gain_key], axis=0
    )
    full_terms = jnp.concatenate([grad_wqkv, grad_wout], axis=1)
    attn_share, gain_share = (
        lax.psum_scatter(full_terms, ("dp", "ep"), scatter_dimension=0, tiled=True),
        lax.psum_scatter(gain_terms, ("dp", "ep"), scatter_dimension=0, tiled=True),
    )
    return (output[None], input_grad[None], attn_share, gain_share, expert_sums[0], expert_sums[1])


def solution(mesh):
    in_specs = (
        P(("dp", "ep"), None, None),
        P(("dp", "ep")),
        P(("dp", "ep"), None, None),
        P(("dp", "ep"), None),
        P(("dp", "ep"), None, None),
        P(("dp", "ep"), None),
        P(),
        P("ep", None, None),
        P("ep", None, None),
        P(("dp", "ep"), None, None),
    )
    out_specs = (
        P(("dp", "ep"), None, None),
        P(("dp", "ep"), None, None),
        P(("dp", "ep"), None),
        P(("dp", "ep")),
        P("ep", "dp", None),
        P("ep", "dp", None),
    )
    return jax.shard_map(
        on_device, mesh=mesh, in_specs=in_specs, out_specs=out_specs, check_vma=False
    )
```

profile of v0, /device:TPU:0, one launch (start us, length us, event | category | flops | bytes accessed | tf_op | source)
XLA Modules:
  0.0 2815.4 jit_solution(5414634431829395121)
XLA Ops:
  11.2 8.0 scatter_custom_fusion
  19.2 13.1 gather_fusion.1
  32.3 11.8 gather_fusion
  44.2 4.6 reduce-window.6
  49.5 11.8 gather_fusion.2
  61.4 8.1 scatter_custom_fusion.1
  73.3 135.3 %all-gather.2.cloned.1.call-done = bf16[2048,8192]{1,0:T(8,128)(2,1)} async-done(((bf16[64,8192]{1,0:T(8,128)(2,1)}), bf16[2048,8192]{1,0:T(8,128)(2,1)}) %all-gather.2.cloned.1.call-update) | async-done | bytes 33554448 | tf_op jit(solution)/shard_map/all_gather | solution.py:88
  208.5 11.7 fusion.2
  220.3 3.4 slice_bitcast_fusion.3
  225.8 1.3 multiply_multiply_fusion.1
  227.1 2.0 copy.253
  230.4 1.3 multiply_multiply_fusion
  231.7 2.7 fusion.62
  234.5 1.5 subtract_convert_fusion.1
  236.0 1.7 fusion.39
  237.9 1.0 exponential_reduce_fusion
  239.8 2.7 convolution_convert_fusion.1
  242.6 6.2 multiply_reduce_fusion.3
  250.2 9.8 gather_fusion.3
  260.0 5.2 all-to-all-start
  266.1 12.3 gather_fusion.6
  279.1 11.5 gather_fusion.5
  290.6 9.9 multiply_convert_fusion
  300.5 171.0 %all-to-all-done = bf16[8,2,144,2048]{3,2,1,0:T(8,128)(2,1)} async-done(((bf16[8,2,144,2048]{3,2,1,0:T(8,128)(2,1)}), bf16[8,2,144,2048]{3,2,1,0:T(8,128)(2,1)}, u32[]{:S(2)}, u32[]{:S(2)}) %all-to-all-start) | async-done | bytes 9437216 | tf_op jit(solution)/shard_map/all_to_all | solution.py:145
  471.5 5.1 all-to-all-start.2
  476.6 27.8 fusion.27
  504.4 177.6 %all-to-all-done.2 = bf16[8,2,144,2048]{3,2,1,0:T(8,128)(2,1)} async-done(((bf16[8,2,144,2048]{3,2,1,0:T(8,128)(2,1)}), bf16[8,2,144,2048]{3,2,1,0:T(8,128)(2,1)}, u32[]{:S(2)}, u32[]{:S(2)}) %all-to-all-start.2) | async-done | bytes 9437216 | tf_op jit(solution)/shard_map/all_to_all | solution.py:179
  682.0 22.7 fusion.11
  704.7 18.3 fusion.32
  723.0 30.6 %convolution_bitcast_fusion = f32[2,2048,2048]{2,1,0:T(8,128)} fusion(bf16[8,2,144,2048]{3,2,1,0:T(8,128)(2,1)} %all-to-all-done, bf16[8,2,144,1024]{3,2,0,1:T(8,128)(2,1)} %get-tuple-element.15, bf16[8,2,144,1024]{3,2,0,1:T(8,128)(2,1)} %get-tuple-element.14), kind=kOutput, calls=%fused_computation.23 | convolution fusion | flops 19346227200 | bytes 52428800 | tf_op jit(solution)/shard_map/sjcd,sjcf->jdf/dot_general | solution.py:192
  753.7 17.2 convert_bitcast_fusion.1
  770.8 9.3 copy.197
  780.1 5.3 all-to-all-start.1
  785.4 25.9 convert_bitcast_fusion
  811.3 9.3 copy.202
  820.6 169.2 %all-to-all-done.1 = bf16[8,2,144,2048]{3,2,1,0:T(8,128)(2,1)} async-done(((bf16[8,2,144,2048]{3,2,1,0:T(8,128)(2,1)}), bf16[8,2,144,2048]{3,2,1,0:T(8,128)(2,1)}, u32[]{:S(2)}, u32[]{:S(2)}) %all-to-all-start.1) | async-done | bytes 9437216 | tf_op jit(solution)/shard_map/all_to_all | solution.py:155
  989.9 5.1 all-to-all-start.3
  997.8 9.3 concatenate.49
  1007.0 192.4 %all-to-all-done.3 = bf16[8,2,144,2048]{3,2,1,0:T(8,128)(2,1)} async-done(((bf16[8,2,144,2048]{3,2,1,0:T(8,128)(2,1)}), bf16[8,2,144,2048]{3,2,1,0:T(8,128)(2,1)}, u32[]{:S(2)}, u32[]{:S(2)}) %all-to-all-start.3) | async-done | bytes 9437216 | tf_op jit(solution)/shard_map/all_to_all | solution.py:198
  1199.4 9.2 concatenate.53
  1208.7 21.3 gather_fusion.4
  1229.9 21.6 gather_fusion.7
  1251.6 11.4 convert_reduce_fusion
  1263.0 2.7 multiply_reduce_fusion.1
  1266.3 12.7 fusion.4
  1279.1 4.1 subtract_add_fusion
  1283.1 1.3 copy-done.3
  1284.5 5.7 fusion.42
  1290.9 3.4 convolution_convert_fusion
  1294.3 1.6 copy.239
  1296.0 4.3 multiply_reduce_fusion
  1300.3 1.4 multiply_convert_fusion.2
  1303.3 1.3 multiply_bitcast_fusion.1
  1304.6 3.1 multiply_add_fusion.1
  1307.8 1.9 fusion.75
  1310.5 4.9 fusion.74
  1316.1 9.9 fusion.76
  1331.3 9.0 fusion.61
  1340.3 21.3 fusion.66
  1361.6 43.4 %pad_maximum_fusion = f32[2048,8192]{1,0:T(8,128)} fusion(f32[2048,2048]{1,0:T(8,128)} %fusion.76, f32[2048,6144]{1,0:T(8,128)} %fusion.66), kind=kLoop, calls=%fused_computation.10 | loop fusion | flops 16777216 | bytes 134217728 | tf_op jit(solution)/shard_map/concatenate | solution.py:266
  1405.1 14.7 fusion.55
  1419.9 47.2 %all-reduce.4 = f32[4352]{0:T(1024)S(1)} all-reduce(f32[4352]{0:T(1024)S(1)} %pad_maximum_fusion.13), channel_id=3, replica_groups=mesh['dp'=4,'ep'=8] {'dp','ep'}, use_global_device_ids=true, to_apply=%region_25.26.clone | all-reduce | flops 4352 | bytes 34816
  1467.7 3.5 fusion.52
  1471.2 1337.2 %reduce-scatter.4.cloned.1.call-done = f32[64,8192]{1,0:T(8,128)} async-done(((f32[2048,8192]{1,0:T(8,128)}), f32[64,8192]{1,0:T(8,128)}) %reduce-scatter.4.cloned.1.call-update) | async-done | bytes 2097168 | tf_op jit(solution)/shard_map/reduce_scatter | solution.py:268
  (224 shorter events, 28.5 us)
Async XLA Ops:
  7.2 201.4 %all-gather.2.cloned.1.call-start = ((), (), s32[]{:S(2)}) async-start(), calls=%async_computation.7 | async-start | bytes 34603008 | tf_op jit(solution)/shard_map/all_gather | solution.py:88
  49.5 21.2 copy-start.9
  49.5 22.0 copy-start.61
  61.3 147.2 %copy-start.43 = (s32[2048]{0:T(1024)}, s32[2048]{0:T(1024)S(1)}, u32[]{:S(2)}) copy-start(s32[2048]{0:T(1024)S(1)} %gather_fusion.2) | copy-start | bytes 24580
  61.4 10.2 copy-start.55
  71.6 137.0 %copy-start.45 = (f32[256]{0:T(256)}, f32[256]{0:T(256)S(1)}, u32[]{:S(2)}) copy-start(f32[256]{0:T(256)S(1)} %get-tuple-element.52) | copy-start | bytes 3076
  72.8 135.8 %copy-start.29 = (f32[2048]{0:T(1024)}, f32[2048]{0:T(1024)S(1)}, u32[]{:S(2)}) copy-start(f32[2048]{0:T(1024)S(1)} %get-tuple-element.42) | copy-start | bytes 24580
  73.3 161.2 %copy-start.25 = (f32[256,64]{1,0:T(8,128)}, f32[256,64]{1,0:T(8,128)S(1)}, u32[]{:S(2)}) copy-start(f32[256,64]{1,0:T(8,128)S(1)} %get-tuple-element.55) | copy-start | bytes 196612
  73.3 161.2 %copy-start.27 = (f32[256,64]{1,0:T(8,128)}, f32[256,64]{1,0:T(8,128)S(1)}, u32[]{:S(2)}) copy-start(f32[256,64]{1,0:T(8,128)S(1)} %get-tuple-element.56) | copy-start | bytes 196612
  220.3 3.8 copy-start.2
  224.1 7.6 copy-start.5
  227.1 4.6 copy-start.36
  231.7 2.7 copy-start.38
  235.9 1.7 copy-start.11
  235.9 1.7 copy-start.13
  236.0 1.7 copy-start.15
  236.0 1.9 copy-start.17
  237.9 1.9 copy-start
  239.8 2.7 copy-start.34
  242.6 6.2 copy-start.21
  242.6 6.9 copy-start.40
  260.0 5.2 copy-start.53
  260.0 5.5 copy-start.44
  260.0 6.1 copy-start.49
  260.0 211.5 %all-to-all-start = ((bf16[8,2,144,2048]{3,2,1,0:T(8,128)(2,1)}), bf16[8,2,144,2048]{3,2,1,0:T(8,128)(2,1)}, u32[]{:S(2)}, u32[]{:S(2)}) async-start(bf16[8,2,144,2048]{3,2,1,0:T(8,128)(2,1)} %bitcast.234), calls=%async_computation | async-start | bytes 18874368 | tf_op jit(solution)/shard_map/all_to_all | solution.py:145
  266.1 12.4 copy-start.23
  266.1 12.4 copy-start.62
  471.5 210.5 %all-to-all-start.2 = ((bf16[8,2,144,2048]{3,2,1,0:T(8,128)(2,1)}), bf16[8,2,144,2048]{3,2,1,0:T(8,128)(2,1)}, u32[]{:S(2)}, u32[]{:S(2)}) async-start(bf16[8,2,144,2048]{3,2,1,0:T(8,128)(2,1)} %multiply_convert_fusion), calls=%async_computation.2 | async-start | bytes 18874368 | tf_op jit(solution)/shard_map/all_to_all | solution.py:179
  476.6 994.7 %reduce-scatter.8.cloned.1.call-start = ((), (), s32[]{:S(2)}) async-start(), calls=%async_computation.10 | async-start | bytes 20971520 | tf_op jit(solution)/shard_map/reduce_scatter | solution.py:213
  723.0 748.3 %reduce-scatter.6.cloned.1.call-start = ((), (), s32[]{:S(2)}) async-start(), calls=%async_computation.9 | async-start | bytes 41943040 | tf_op jit(solution)/shard_map/reduce_scatter | solution.py:212
  780.1 209.8 %all-to-all-start.1 = ((bf16[8,2,144,2048]{3,2,1,0:T(8,128)(2,1)}), bf16[8,2,144,2048]{3,2,1,0:T(8,128)(2,1)}, u32[]{:S(2)}, u32[]{:S(2)}) async-start(bf16[8,2,144,2048]{3,2,1,0:T(8,128)(2,1)} %copy.197), calls=%async_computation.1 | async-start | bytes 18874368 | tf_op jit(solution)/shard_map/all_to_all | solution.py:155
  820.6 174.5 %copy-start.68 = (pred[2048]{0:T(1024)(128)(4,1)S(1)}, pred[2048]{0:T(1024)(128)(4,1)}, u32[]{:S(2)}) copy-start(pred[2048]{0:T(1024)(128)(4,1)} %get-tuple-element.13) | copy-start | bytes 6148
  820.6 174.7 %copy-start.54 = (f32[1,256,8]{1,2,0:T(8,128)S(1)}, f32[1,256,8]{1,2,0:T(8,128)}, u32[]{:S(2)}) copy-start(f32[1,256,8]{1,2,0:T(8,128)} %param.14) | copy-start | bytes 24580
  820.6 175.5 %copy-start.56 = (s32[2048,1]{0,1:T(1,128)S(1)}, s32[2048,1]{0,1:T(1,128)}, u32[]{:S(2)}) copy-start(s32[2048,1]{0,1:T(1,128)} %copy-done.55) | copy-start | bytes 24580
  820.6 175.5 %copy-start.64 = (f32[128]{0:T(128)S(1)}, f32[128]{0:T(128)}, u32[]{:S(2)}) copy-start(f32[128]{0:T(128)} %get-tuple-element.44) | copy-start | bytes 1540
  820.6 175.5 %copy-start.66 = (f32[128]{0:T(128)S(1)}, f32[128]{0:T(128)}, u32[]{:S(2)}) copy-start(f32[128]{0:T(128)} %get-tuple-element.43) | copy-start | bytes 1540
  820.6 176.1 %copy-start.37 = (f32[256,16]{0,1:T(8,128)S(1)}, f32[256,16]{0,1:T(8,128)}, u32[]{:S(2)}) copy-start(f32[256,16]{0,1:T(8,128)} %copy-done.36) | copy-start | bytes 49156
  820.6 176.2 %copy-start.39 = (f32[256,16]{0,1:T(8,128)S(1)}, f32[256,16]{0,1:T(8,128)}, u32[]{:S(2)}) copy-start(f32[256,16]{0,1:T(8,128)} %copy-done.38) | copy-start | bytes 49156
  820.6 176.3 %copy-start.47 = (f32[256,16]{0,1:T(8,128)S(1)}, f32[256,16]{0,1:T(8,128)}, u32[]{:S(2)}) copy-start(f32[256,16]{0,1:T(8,128)} %get-tuple-element.45) | copy-start | bytes 49156
  820.6 177.0 %copy-start.48 = (f32[256,16]{0,1:T(8,128)S(1)}, f32[256,16]{0,1:T(8,128)}, u32[]{:S(2)}) copy-start(f32[256,16]{0,1:T(8,128)} %get-tuple-element.47) | copy-start | bytes 49156
  989.9 209.5 %all-to-all-start.3 = ((bf16[8,2,144,2048]{3,2,1,0:T(8,128)(2,1)}), bf16[8,2,144,2048]{3,2,1,0:T(8,128)(2,1)}, u32[]{:S(2)}, u32[]{:S(2)}) async-start(bf16[8,2,144,2048]{3,2,1,0:T(8,128)(2,1)} %copy.202), calls=%async_computation.3 | async-start | bytes 18874368 | tf_op jit(solution)/shard_map/all_to_all | solution.py:198
  995.0 1813.4 %reduce-scatter.4.cloned.1.call-start = ((), (), s32[]{:S(2)}) async-start(), calls=%async_computation.8 | async-start | bytes 69206016 | tf_op jit(solution)/shard_map/reduce_scatter | solution.py:268
  1251.6 11.4 copy-start.8
  1251.6 11.4 copy-start.41
  1251.6 11.4 copy-start.60
  1266.3 12.7 copy-start.24
  1266.3 12.7 copy-start.63
  1296.0 4.3 copy-start.1
  1304.6 3.1 copy-start.6
  1304.6 3.1 copy-start.67
  1307.8 2.7 copy-start.65
  1310.5 5.7 copy-start.22
  1310.5 19.8 slice-start
  1316.1 14.2 slice-start.1
  1329.0 1.6 copy-start.19
  1329.1 2.2 copy-start.20
  1329.1 2.2 copy-start.51
  1329.1 2.2 copy-start.52
  1331.3 9.0 copy-start.10
  1331.3 9.0 copy-start.30
  1331.3 9.0 copy-start.46
  1405.1 14.8 copy-start.50
  1405.1 62.6 %copy-start.4 = (f32[256,2048]{1,0:T(8,128)S(1)}, f32[256,2048]{1,0:T(8,128)}, u32[]{:S(2)}) copy-start(f32[256,2048]{1,0:T(8,128)} %copy-done.3) | copy-start | bytes 6291460
  1405.1 62.6 %copy-start.69 = (f32[256]{0:T(256)S(1)}, f32[256]{0:T(256)}, u32[]{:S(2)}) copy-start(f32[256]{0:T(256)} %get-tuple-element.51) | copy-start | bytes 3076
  (16 other events, 19.1 us)
Sparse Core Ops, SparseCore 0:
  11.0 197.5 all-gather.1
  723.1 125.1 reduce-scatter.7
  851.6 234.8 reduce-scatter.5
  1405.2 1403.1 reduce-scatter.3
where the time goes:
time: 2820 us
  waiting for transfers between devices  2180 us (77%)
  matrix products  226 us (8%)
  local copies, waits for them, and re-layouts  194 us (7%)
  other arithmetic  128 us (5%)
  blocking collectives  47.2 us (2%)
    reduce_scatter x1, waiting for transfers between devices, on_device(): lax.psum_scatter(full_terms, ('dp', 'ep'), scatter_dimension=0, tiled=True)  1340 us
    all_to_all x1, waiting for transfers between devices, on_device(): lax.all_to_all(grad_rows.astype(jnp.bfloat16), 'ep', split_axis=0, concat...  192 us
    all_to_all x1, waiting for transfers between devices, on_device(): lax.all_to_all(slot_grad, 'ep', split_axis=0, concat_axis=0, tiled=True)  178 us
    all_to_all x1, waiting for transfers between devices, on_device(): lax.all_to_all(send_rows, 'ep', split_axis=0, concat_axis=0, tiled=True)  171 us
    all_to_all x1, waiting for transfers between devices, on_device(): lax.all_to_all(result.astype(jnp.bfloat16), 'ep', split_axis=0, concat_ax...  169 us
    all_gather x1, waiting for transfers between devices, on_device(): whole_weight = lax.all_gather(attn_weight, ('dp', 'ep'), axis=0, tiled=True)  135 us
  transfers between devices with their start and end apart: 8, of which 6 were waited for; matrix products, arithmetic and copies ran while one was open for 16% of the time, Pallas kernels for 0%

commit v1 on v0

--- a/solution.py
+++ b/solution.py
@@ -8,6 +8,18 @@
 EPS = 1e-06
 THETA = 10000.0
 NEG = -1e30
+
+
+def collect(value, axis, dim):
+    ways, here, lap = (lax.axis_size(axis), lax.axis_index(axis), value.shape[dim])
+    line, have = (value, 1)
+    while have < ways:
+        line = jnp.concatenate(
+            [line, lax.ppermute(line, axis, [(d, (d - have) % ways) for d in range(ways)])],
+            axis=dim,
+        )
+        have = 2 * have
+    return jnp.roll(line, here * lap, axis=dim)
 
 
 def inv_rms(values):
@@ -85,7 +97,7 @@
     gain_ffn = gains[model_width : 2 * model_width]
     gain_query = gains[2 * model_width : 2 * model_width + head_size]
     gain_key = gains[2 * model_width + head_size :]
-    whole_weight = lax.all_gather(attn_weight, ("dp", "ep"), axis=0, tiled=True)
+    whole_weight = collect(attn_weight, ("dp", "ep"), 0)
     weight_qkv = whole_weight[:, : 3 * model_width]
     weight_out = whole_weight[:, 3 * model_width :]
     scale_first = inv_rms(inputs)

time: 2820 us -> 3390 us (1.20)
  waiting for transfers between devices: 2180 us -> 2680 us
  local copies, waits for them, and re-layouts: 194 us -> 253 us
    ppermute x0 -> x5, waiting for transfers between devices: none -> 631 us  [collect(): lax.ppermute(line, axis, [(d, (d - have) % ways) for d in range(ways)])]
    all_gather x1 -> x0, waiting for transfers between devices: 135 us -> none  [on_device(): whole_weight = lax.all_gather(attn_weight, ('dp', 'ep'), axis=0, tiled=True)]
    unnamed x152 -> x178, local copies, waits for them, and re-layouts: 13.2 us -> 49.1 us
  transfers between devices with their start and end apart: 8 -> 12, of which waited for: 6 -> 10; matrix products, arithmetic and copies ran while one was open for 16% -> 14% of each run, Pallas kernels for 0% -> 0%
where the time goes in v1:
time: 3390 us
  waiting for transfers between devices  2680 us (79%)
  local copies, waits for them, and re-layouts  253 us (7%)
  matrix products  229 us (7%)
  other arithmetic  135 us (4%)
  blocking collectives  50 us (1%)
    reduce_scatter x1, waiting for transfers between devices, on_device(): lax.psum_scatter(full_terms, ('dp', 'ep'), scatter_dimension=0, tiled=True)  1330 us
    ppermute x5, waiting for transfers between devices, collect(): lax.ppermute(line, axis, [(d, (d - have) % ways) for d in range(ways)])  631 us
    all_to_all x1, waiting for transfers between devices, on_device(): lax.all_to_all(grad_rows.astype(jnp.bfloat16), 'ep', split_axis=0, concat...  192 us
    all_to_all x1, waiting for transfers between devices, on_device(): lax.all_to_all(slot_grad, 'ep', split_axis=0, concat_axis=0, tiled=True)  178 us
    all_to_all x1, waiting for transfers between devices, on_device(): lax.all_to_all(send_rows, 'ep', split_axis=0, concat_axis=0, tiled=True)  171 us
    all_to_all x1, waiting for transfers between devices, on_device(): lax.all_to_all(result.astype(jnp.bfloat16), 'ep', split_axis=0, concat_ax...  169 us
  transfers between devices with their start and end apart: 12, of which 10 were waited for; matrix products, arithmetic and copies ran while one was open for 14% of the time, Pallas kernels for 0%

profile of v1, /device:TPU:0, one launch (start us, length us, event | category | flops | bytes accessed | tf_op | source)
XLA Modules:
  0.0 3387.7 jit_solution(8972432696100122534)
XLA Ops:
  7.2 6.4 collective-permute-start
  13.6 22.9 collective-permute-done
  38.8 46.3 %collective-permute-done.1 = bf16[128,8192]{1,0:T(8,128)(2,1)S(1)} collective-permute-done((bf16[128,8192]{1,0:T(8,128)(2,1)S(1)}, bf16[128,8192]{1,0:T(8,128)(2,1)S(1)}, u32[]{:S(2)}, u32[]{:S(2)}) %collective-permute-start.1) | collective-permute-done | bytes 2097184 | tf_op jit(solution)/shard_map/ppermute | solution.py:18
  85.5 182.9 %collective-permute-done.2 = bf16[256,8192]{1,0:T(8,128)(2,1)S(1)} collective-permute-done((bf16[256,8192]{1,0:T(8,128)(2,1)S(1)}, bf16[256,8192]{1,0:T(8,128)(2,1)S(1)}, u32[]{:S(2)}, u32[]{:S(2)}) %collective-permute-start.2) | collective-permute-done | bytes 4194336 | tf_op jit(solution)/shard_map/ppermute | solution.py:18
  268.4 4.3 pad_maximum_fusion.2
  279.2 4.2 constant_dynamic-update-slice_fusion.1
  283.5 81.5 %collective-permute-done.3 = bf16[512,8192]{1,0:T(8,128)(2,1)S(1)} collective-permute-done((bf16[512,8192]{1,0:T(8,128)(2,1)}, bf16[512,8192]{1,0:T(8,128)(2,1)S(1)}, u32[]{:S(2)}, u32[]{:S(2)}) %collective-permute-start.3) | collective-permute-done | bytes 8388640 | tf_op jit(solution)/shard_map/ppermute | solution.py:18
  365.0 7.3 constant_dynamic-update-slice_fusion
  375.5 8.0 scatter_custom_fusion
  383.6 13.1 gather_fusion.1
  396.7 11.8 gather_fusion
  408.5 4.5 reduce-window.6
  414.2 11.8 gather_fusion.2
  426.0 8.6 scatter_custom_fusion.1
  439.6 297.0 %collective-permute-done.4 = bf16[1024,8192]{1,0:T(8,128)(2,1)} collective-permute-done((bf16[1024,8192]{1,0:T(8,128)(2,1)}, bf16[1024,8192]{1,0:T(8,128)(2,1)}, u32[]{:S(2)}, u32[]{:S(2)}) %collective-permute-start.4) | collective-permute-done | bytes 16777248 | tf_op jit(solution)/shard_map/ppermute | solution.py:18
  736.6 14.0 constant_dynamic-update-slice_fusion.11
  756.6 7.6 constant_dynamic-update-slice_fusion.6
  764.2 14.0 constant_dynamic-update-slice_fusion.5
  778.2 11.7 fusion.2
  789.9 3.5 slice_bitcast_fusion.3
  801.5 2.7 fusion.62
  808.7 3.2 convolution_convert_fusion.1
  811.9 6.2 multiply_reduce_fusion.3
  819.8 9.9 gather_fusion.3
  829.7 6.1 all-to-all-start
  836.7 12.3 gather_fusion.6
  849.6 11.5 gather_fusion.5
  861.1 9.9 multiply_convert_fusion
  871.0 171.4 %all-to-all-done = bf16[8,2,144,2048]{3,2,1,0:T(8,128)(2,1)} async-done(((bf16[8,2,144,2048]{3,2,1,0:T(8,128)(2,1)}), bf16[8,2,144,2048]{3,2,1,0:T(8,128)(2,1)}, u32[]{:S(2)}, u32[]{:S(2)}) %all-to-all-start) | async-done | bytes 9437216 | tf_op jit(solution)/shard_map/all_to_all | solution.py:157
  1042.4 5.1 all-to-all-start.2
  1047.6 27.5 fusion.27
  1075.1 178.1 %all-to-all-done.2 = bf16[8,2,144,2048]{3,2,1,0:T(8,128)(2,1)} async-done(((bf16[8,2,144,2048]{3,2,1,0:T(8,128)(2,1)}), bf16[8,2,144,2048]{3,2,1,0:T(8,128)(2,1)}, u32[]{:S(2)}, u32[]{:S(2)}) %all-to-all-start.2) | async-done | bytes 9437216 | tf_op jit(solution)/shard_map/all_to_all | solution.py:191
  1253.2 22.8 fusion.11
  1276.0 18.5 fusion.32
  1294.6 31.7 convolution_bitcast_fusion
  1326.3 16.4 convert_bitcast_fusion.1
  1342.7 9.3 copy.197
  1352.1 5.2 all-to-all-start.1
  1357.3 25.7 convert_bitcast_fusion
  1383.0 9.5 copy.202
  1392.5 169.3 %all-to-all-done.1 = bf16[8,2,144,2048]{3,2,1,0:T(8,128)(2,1)} async-done(((bf16[8,2,144,2048]{3,2,1,0:T(8,128)(2,1)}), bf16[8,2,144,2048]{3,2,1,0:T(8,128)(2,1)}, u32[]{:S(2)}, u32[]{:S(2)}) %all-to-all-start.1) | async-done | bytes 9437216 | tf_op jit(solution)/shard_map/all_to_all | solution.py:167
  1561.8 5.1 all-to-all-start.3
  1569.7 9.4 concatenate.76
  1579.1 192.2 %all-to-all-done.3 = bf16[8,2,144,2048]{3,2,1,0:T(8,128)(2,1)} async-done(((bf16[8,2,144,2048]{3,2,1,0:T(8,128)(2,1)}), bf16[8,2,144,2048]{3,2,1,0:T(8,128)(2,1)}, u32[]{:S(2)}, u32[]{:S(2)}) %all-to-all-start.3) | async-done | bytes 9437216 | tf_op jit(solution)/shard_map/all_to_all | solution.py:210
  1771.3 9.3 concatenate.80
  1780.6 21.2 gather_fusion.4
  1801.8 21.5 gather_fusion.7
  1823.3 11.5 convert_reduce_fusion
  1834.8 2.7 multiply_reduce_fusion.1
  1838.0 13.0 fusion.4
  1851.0 4.1 subtract_add_fusion
  1856.4 5.8 fusion.42
  1862.9 4.3 multiply_reduce_fusion
  1871.6 3.1 multiply_add_fusion.1
  1878.8 4.2 fusion.75
  1883.7 4.5 convolution_convert_fusion
  1890.7 10.2 fusion.76
  1904.6 9.0 fusion.61
  1913.6 21.6 fusion.66
  1935.2 43.3 %pad_maximum_fusion = f32[2048,8192]{1,0:T(8,128)} fusion(f32[2048,2048]{1,0:T(8,128)} %fusion.76, f32[2048,6144]{1,0:T(8,128)} %fusion.66), kind=kLoop, calls=%fused_computation.10 | loop fusion | flops 16777216 | bytes 134217728 | tf_op jit(solution)/shard_map/concatenate | solution.py:278
  1978.6 14.7 fusion.55
  1993.3 50.0 %all-reduce.4 = f32[4352]{0:T(1024)S(1)} all-reduce(f32[4352]{0:T(1024)S(1)} %pad_maximum_fusion.16), channel_id=3, replica_groups=mesh['dp'=4,'ep'=8] {'dp','ep'}, use_global_device_ids=true, to_apply=%region_25.26.clone | all-reduce | flops 4352 | bytes 34816
  2044.0 3.5 fusion.52
  2047.5 1333.5 %reduce-scatter.4.cloned.1.call-done = f32[64,8192]{1,0:T(8,128)} async-done(((f32[2048,8192]{1,0:T(8,128)}), f32[64,8192]{1,0:T(8,128)}) %reduce-scatter.4.cloned.1.call-update) | async-done | bytes 2097168 | tf_op jit(solution)/shard_map/reduce_scatter | solution.py:280
  (262 shorter events, 60.6 us)
Async XLA Ops:
  7.2 77.9 %copy-start.5 = (bf16[64,8192]{1,0:T(8,128)(2,1)S(1)}, bf16[64,8192]{1,0:T(8,128)(2,1)}, u32[]{:S(2)}) copy-start(bf16[64,8192]{1,0:T(8,128)(2,1)} %param.15) | copy-start | bytes 3145732
  7.2 29.3 collective-permute-start
  36.5 238.7 %copy-start.6 = (bf16[64,8192]{1,0:T(8,128)(2,1)}, bf16[64,8192]{1,0:T(8,128)(2,1)S(1)}, u32[]{:S(2)}) copy-start(bf16[64,8192]{1,0:T(8,128)(2,1)S(1)} %collective-permute-done) | copy-start | bytes 3145732
  38.3 46.7 %collective-permute-start.1 = (bf16[128,8192]{1,0:T(8,128)(2,1)S(1)}, bf16[128,8192]{1,0:T(8,128)(2,1)S(1)}, u32[]{:S(2)}, u32[]{:S(2)}) collective-permute-start(bf16[128,8192]{1,0:T(8,128)(2,1)S(1)} %pad_maximum_fusion.5), channel_id=1, source_target_pairs={{0,30},{1,31},{2,0},{3,1},{4,2},{5,3},{6,4},{7,5},{8,6},{9,7},{10,... | collective-permute-start | bytes 6291464 | tf_op jit(solution)/shard_map/ppermute | solution.py:18
  85.4 183.0 %collective-permute-start.2 = (bf16[256,8192]{1,0:T(8,128)(2,1)S(1)}, bf16[256,8192]{1,0:T(8,128)(2,1)S(1)}, u32[]{:S(2)}, u32[]{:S(2)}) collective-permute-start(bf16[256,8192]{1,0:T(8,128)(2,1)S(1)} %pad_maximum_fusion.3), channel_id=1, source_target_pairs={{0,28},{1,29},{2,30},{3,31},{4,0},{5,1},{6,2},{7,3},{8,4},{9,5},{1... | collective-permute-start | bytes 12582920 | tf_op jit(solution)/shard_map/ppermute | solution.py:18
  268.4 10.8 copy-start.2
  272.7 92.3 %collective-permute-start.3 = (bf16[512,8192]{1,0:T(8,128)(2,1)}, bf16[512,8192]{1,0:T(8,128)(2,1)S(1)}, u32[]{:S(2)}, u32[]{:S(2)}) collective-permute-start(bf16[512,8192]{1,0:T(8,128)(2,1)} %pad_maximum_fusion.2), channel_id=1, source_target_pairs={{0,24},{1,25},{2,26},{3,27},{4,28},{5,29},{6,30},{7,31},{8,0},{9,1... | collective-permute-start | bytes 25165832 | tf_op jit(solution)/shard_map/ppermute | solution.py:18
  365.0 8.4 copy-start.4
  365.0 10.3 copy-start.60
  365.0 10.5 copy-start.75
  373.4 363.1 %collective-permute-start.4 = (bf16[1024,8192]{1,0:T(8,128)(2,1)}, bf16[1024,8192]{1,0:T(8,128)(2,1)}, u32[]{:S(2)}, u32[]{:S(2)}) collective-permute-start(bf16[1024,8192]{1,0:T(8,128)(2,1)} %get-tuple-element.19), channel_id=1, source_target_pairs={{0,16},{1,17},{2,18},{3,19},{4,20},{5,21},{6,22},{7,23},{8,24},{9,... | collective-permute-start | bytes 50331656 | tf_op jit(solution)/shard_map/ppermute | solution.py:18
  414.2 23.8 copy-start.67
  426.0 12.5 copy-start.48
  426.0 12.4 copy-start.61
  435.2 373.5 %copy-start.63 = (pred[256]{0:T(512)(128)(4,1)}, pred[256]{0:T(512)(128)(4,1)S(1)}, u32[]{:S(2)}) copy-start(pred[256]{0:T(512)(128)(4,1)S(1)} %get-tuple-element.74) | copy-start | bytes 772
  437.9 340.2 %copy-start.50 = (f32[256]{0:T(256)}, f32[256]{0:T(256)S(1)}, u32[]{:S(2)}) copy-start(f32[256]{0:T(256)S(1)} %get-tuple-element.62) | copy-start | bytes 3076
  439.1 339.1 %copy-start.35 = (f32[2048]{0:T(1024)}, f32[2048]{0:T(1024)S(1)}, u32[]{:S(2)}) copy-start(f32[2048]{0:T(1024)S(1)} %get-tuple-element.52) | copy-start | bytes 24580
  439.6 364.7 %copy-start.31 = (f32[256,64]{1,0:T(8,128)}, f32[256,64]{1,0:T(8,128)S(1)}, u32[]{:S(2)}) copy-start(f32[256,64]{1,0:T(8,128)S(1)} %get-tuple-element.65) | copy-start | bytes 196612
  439.6 364.7 %copy-start.33 = (f32[256,64]{1,0:T(8,128)}, f32[256,64]{1,0:T(8,128)S(1)}, u32[]{:S(2)}) copy-start(f32[256,64]{1,0:T(8,128)S(1)} %get-tuple-element.66) | copy-start | bytes 196612
  736.6 15.1 copy-start.7
  764.2 14.0 copy-start.16
  793.9 7.6 copy-start.11
  794.3 7.3 copy-start.70
  794.3 7.3 copy-start.72
  811.9 6.2 copy-start.28
  811.9 7.6 copy-start.45
  829.7 6.1 copy-start.58
  829.7 6.4 copy-start.49
  829.7 7.0 copy-start.54
  829.7 212.7 %all-to-all-start = ((bf16[8,2,144,2048]{3,2,1,0:T(8,128)(2,1)}), bf16[8,2,144,2048]{3,2,1,0:T(8,128)(2,1)}, u32[]{:S(2)}, u32[]{:S(2)}) async-start(bf16[8,2,144,2048]{3,2,1,0:T(8,128)(2,1)} %bitcast.232), calls=%async_computation | async-start | bytes 18874368 | tf_op jit(solution)/shard_map/all_to_all | solution.py:157
  836.7 12.4 copy-start.29
  836.7 12.4 copy-start.68
  1042.4 210.8 %all-to-all-start.2 = ((bf16[8,2,144,2048]{3,2,1,0:T(8,128)(2,1)}), bf16[8,2,144,2048]{3,2,1,0:T(8,128)(2,1)}, u32[]{:S(2)}, u32[]{:S(2)}) async-start(bf16[8,2,144,2048]{3,2,1,0:T(8,128)(2,1)} %multiply_convert_fusion), calls=%async_computation.2 | async-start | bytes 18874368 | tf_op jit(solution)/shard_map/all_to_all | solution.py:191
  1047.5 999.9 %reduce-scatter.8.cloned.1.call-start = ((), (), s32[]{:S(2)}) async-start(), calls=%async_computation.9 | async-start | bytes 20971520 | tf_op jit(solution)/shard_map/reduce_scatter | solution.py:225
  1294.5 753.0 %reduce-scatter.6.cloned.1.call-start = ((), (), s32[]{:S(2)}) async-start(), calls=%async_computation.8 | async-start | bytes 41943040 | tf_op jit(solution)/shard_map/reduce_scatter | solution.py:224
  1352.1 209.8 %all-to-all-start.1 = ((bf16[8,2,144,2048]{3,2,1,0:T(8,128)(2,1)}), bf16[8,2,144,2048]{3,2,1,0:T(8,128)(2,1)}, u32[]{:S(2)}, u32[]{:S(2)}) async-start(bf16[8,2,144,2048]{3,2,1,0:T(8,128)(2,1)} %copy.197), calls=%async_computation.1 | async-start | bytes 18874368 | tf_op jit(solution)/shard_map/all_to_all | solution.py:167
  1392.5 174.5 %copy-start.76 = (pred[2048]{0:T(1024)(128)(4,1)S(1)}, pred[2048]{0:T(1024)(128)(4,1)}, u32[]{:S(2)}) copy-start(pred[2048]{0:T(1024)(128)(4,1)} %get-tuple-element.13) | copy-start | bytes 6148
  1392.5 174.7 %copy-start.59 = (f32[1,256,8]{1,2,0:T(8,128)S(1)}, f32[1,256,8]{1,2,0:T(8,128)}, u32[]{:S(2)}) copy-start(f32[1,256,8]{1,2,0:T(8,128)} %param.14) | copy-start | bytes 24580
  1392.5 175.6 %copy-start.62 = (s32[2048,1]{0,1:T(1,128)S(1)}, s32[2048,1]{0,1:T(1,128)}, u32[]{:S(2)}) copy-start(s32[2048,1]{0,1:T(1,128)} %copy-done.61) | copy-start | bytes 24580
  1392.5 175.6 %copy-start.71 = (f32[128]{0:T(128)S(1)}, f32[128]{0:T(128)}, u32[]{:S(2)}) copy-start(f32[128]{0:T(128)} %get-tuple-element.53) | copy-start | bytes 1540
  1392.5 175.6 %copy-start.73 = (f32[128]{0:T(128)S(1)}, f32[128]{0:T(128)}, u32[]{:S(2)}) copy-start(f32[128]{0:T(128)} %get-tuple-element.54) | copy-start | bytes 1540
  1392.5 176.2 %copy-start.42 = (f32[256,16]{0,1:T(8,128)S(1)}, f32[256,16]{0,1:T(8,128)}, u32[]{:S(2)}) copy-start(f32[256,16]{0,1:T(8,128)} %get-tuple-element.56) | copy-start | bytes 49156
  1392.5 176.2 %copy-start.44 = (f32[256,16]{0,1:T(8,128)S(1)}, f32[256,16]{0,1:T(8,128)}, u32[]{:S(2)}) copy-start(f32[256,16]{0,1:T(8,128)} %copy-done.43) | copy-start | bytes 49156
  1392.5 176.3 %copy-start.52 = (f32[256,16]{0,1:T(8,128)S(1)}, f32[256,16]{0,1:T(8,128)}, u32[]{:S(2)}) copy-start(f32[256,16]{0,1:T(8,128)} %get-tuple-element.55) | copy-start | bytes 49156
  1392.5 177.1 %copy-start.53 = (f32[256,16]{0,1:T(8,128)S(1)}, f32[256,16]{0,1:T(8,128)}, u32[]{:S(2)}) copy-start(f32[256,16]{0,1:T(8,128)} %get-tuple-element.57) | copy-start | bytes 49156
  1561.8 209.4 %all-to-all-start.3 = ((bf16[8,2,144,2048]{3,2,1,0:T(8,128)(2,1)}), bf16[8,2,144,2048]{3,2,1,0:T(8,128)(2,1)}, u32[]{:S(2)}, u32[]{:S(2)}) async-start(bf16[8,2,144,2048]{3,2,1,0:T(8,128)(2,1)} %copy.202), calls=%async_computation.3 | async-start | bytes 18874368 | tf_op jit(solution)/shard_map/all_to_all | solution.py:210
  1566.9 1814.0 %reduce-scatter.4.cloned.1.call-start = ((), (), s32[]{:S(2)}) async-start(), calls=%async_computation.7 | async-start | bytes 69206016 | tf_op jit(solution)/shard_map/reduce_scatter | solution.py:280
  1823.3 11.5 copy-start.15
  1823.3 11.5 copy-start.46
  1823.3 11.5 copy-start.66
  1838.0 13.0 copy-start.30
  1838.0 13.0 copy-start.69
  1856.4 6.5 copy-start.41
  1856.4 6.5 copy-start.64
  1883.7 20.9 slice-start
  1890.7 10.2 copy-start.38
  1890.7 10.8 copy-start.39
  1890.7 13.9 slice-start.1
  1904.6 9.0 copy-start.17
  1904.6 9.0 copy-start.36
  1904.6 9.0 copy-start.51
  1978.6 14.8 copy-start.55
  1978.6 65.4 %copy-start.10 = (f32[256,2048]{1,0:T(8,128)S(1)}, f32[256,2048]{1,0:T(8,128)}, u32[]{:S(2)}) copy-start(f32[256,2048]{1,0:T(8,128)} %copy-done.9) | copy-start | bytes 6291460
  1978.6 65.4 %copy-start.77 = (f32[256]{0:T(256)S(1)}, f32[256]{0:T(256)}, u32[]{:S(2)}) copy-start(f32[256]{0:T(256)} %get-tuple-element.61) | copy-start | bytes 3076
  (28 other events, 64.8 us)
Sparse Core Ops, SparseCore 0:
  1294.6 124.2 reduce-scatter.7
  1422.2 234.8 reduce-scatter.5
  1978.6 1402.2 reduce-scatter.3
